TPU v7x, 32 devices: a whole 2x2x4 slice. The times are simulated.
32 devices in a mesh: expert: 4 (over z), batch: 8 (over y, x, core).
Axes of the slice: x: 2, y: 2, z: 4, core: 2. Of those that a mesh axis runs over, the one named last changes fastest.
Arguments:
- tokens: bfloat16 [32, 1024, 768], P(('expert', 'batch')), may hold values from -6 to 6
- lengths: int32 [32], P(('expert', 'batch')), may hold values from 64 to 1024, as said below
- routes: int32 [32, 1024, 2], P(('expert', 'batch')), may hold values from 0 to 7, as said below
- ln1_gain: float32 [768], replicated, may hold values from 0.5 to 1.5
- ln1_bias: float32 [768], replicated, may hold values from -1.5 to 1.5
- ln2_gain: float32 [768], replicated, may hold values from 0.5 to 1.5
- ln2_bias: float32 [768], replicated, may hold values from -1.5 to 1.5
- w_qkv: bfloat16 [768, 2304], replicated, may hold values from -0.21875 to 0.21875
- w_proj: bfloat16 [768, 768], replicated, may hold values from -1.25 to 1.25
- w_router: bfloat16 [768, 8], replicated, may hold values from -0.15625 to 0.15625
- old_in: bfloat16 [4, 768, 3072], P('expert', 'batch'), may hold values from -0.21875 to 0.21875
- old_out: bfloat16 [4, 3072, 768], P('expert', 'batch'), may hold values from -0.109375 to 0.109375
- new_in: bfloat16 [4, 768, 3072], P('expert', 'batch'), may hold values from -0.21875 to 0.21875
- new_out: bfloat16 [4, 3072, 768], P('expert', 'batch'), may hold values from -0.109375 to 0.109375
- cotangent: bfloat16 [32, 1024, 768], P(('expert', 'batch')), may hold values from -6 to 6
Outputs:
- output: float32 [32, 1024, 768], P(('expert', 'batch'))
- input_grad: float32 [32, 1024, 768], P(('expert', 'batch'))
- ln1_gain_grad: float32 [768], replicated
- ln1_bias_grad: float32 [768], replicated
- ln2_gain_grad: float32 [768], replicated
- ln2_bias_grad: float32 [768], replicated
- qkv_grad: float32 [768, 2304], replicated
- proj_grad: float32 [768, 768], replicated
- router_grad: float32 [768, 8], replicated
- new_in_grad: float32 [4, 768, 3072], P('expert', 'batch')
- new_out_grad: float32 [4, 3072, 768], P('expert', 'batch')
Inputs may be any that keep to these rules, and one draw needn't show every extreme that they name: Positions lengths[r] and beyond of row r are padding. In every draw some row has 1024 tokens and some row 64. `routes`: the two experts of one token always differ. Across the tokens of a sequence row the same expert is named many times, and some experts are named more often than others.
All inputs are finite; a program needn't handle non-finite values.
Results may differ from a plain program's by a relative error of at most 0.012.
Values may be sent and summed in bfloat16 or wider, within the bound.
No kernel may reach another device: no remote copies, remote signals or barrier semaphores. Data moves between devices by JAX's collectives and lax.ppermute only.
A program may use at most 320 MiB of HBM per device.

v0:
```python
import math
import jax
import jax.numpy as jnp
from jax import lax
from jax.sharding import PartitionSpec as P

HEADS = 12
HEAD_DIM = 64
norm_eps = 1e-05
masked_value = -1e30


def layer_norm(field_in, gain_vec, bias_vec):
    row_mean = jnp.mean(field_in, axis=-1, keepdims=True)
    centred = field_in - row_mean
    row_var = jnp.mean(centred * centred, axis=-1, keepdims=True)
    return centred * lax.rsqrt(row_var + norm_eps) * gain_vec + bias_vec


def gelu_tanh(field_in):
    inner_arg = 0.7978845608028654 * (field_in + 0.044715 * field_in * field_in * field_in)
    return 0.5 * field_in * (1.0 + jnp.tanh(inner_arg))


def rank_pairs(route_row, length, experts, capacity):
    seq_len = route_row.shape[0]
    pair_expert = jnp.transpose(route_row).reshape(2 * seq_len)
    live_pair = jnp.tile(jnp.arange(seq_len, dtype=jnp.int32) < length, 2)
    one_hot = (pair_expert[:, None] == jnp.arange(experts, dtype=jnp.int32)[None, :]).astype(
        jnp.int32
    ) * live_pair[:, None].astype(jnp.int32)
    earlier = jnp.cumsum(one_hot, axis=0, dtype=jnp.int32) - one_hot
    pair_rank = jnp.sum(earlier * one_hot, axis=1, dtype=jnp.int32)
    kept_pair = live_pair & (pair_rank < capacity)
    return (
        jnp.transpose(pair_rank.reshape(2, seq_len)),
        jnp.transpose(kept_pair.reshape(2, seq_len)),
    )


def buffer_row(expert_ids, experts, group_size):
    half_count = experts // 2
    per_device = half_count // group_size
    is_new = expert_ids >= half_count
    within = jnp.where(is_new, expert_ids - half_count, expert_ids)
    extra = jnp.where(is_new, per_device, 0).astype(jnp.int32)
    return within // per_device * (2 * per_device) + extra + within % per_device


def expert_hidden(buffer_rows, weights_in):
    pre_act = jnp.einsum(
        "slcd,ldf->slcf", buffer_rows, weights_in, preferred_element_type=jnp.float32
    )
    return (pre_act, gelu_tanh(pre_act).astype(jnp.bfloat16))


def expert_output(hidden, weights_out):
    return jnp.einsum("slcf,lfd->slcd", hidden, weights_out, preferred_element_type=jnp.float32)


def expert_back(pre_act, grads_out, weights_out):
    hid_grad = jnp.einsum(
        "slcd,lfd->slcf", grads_out, weights_out, preferred_element_type=jnp.float32
    )
    unused, gelu_back = jax.vjp(gelu_tanh, pre_act)
    return gelu_back(hid_grad)[0].astype(jnp.bfloat16)


def row_grads_of(pre_grad, weights_in):
    return jnp.einsum("slcf,ldf->slcd", pre_grad, weights_in, preferred_element_type=jnp.float32)


def body(
    tokens,
    lengths,
    routes,
    ln1_gain,
    ln1_bias,
    ln2_gain,
    ln2_bias,
    w_qkv,
    w_proj,
    w_router,
    old_in,
    old_out,
    new_in,
    new_out,
    cotangent,
):
    group_size = lax.axis_size("expert")
    inputs = tokens[0].astype(jnp.float32)
    seq_len = inputs.shape[0]
    model_width = inputs.shape[1]
    experts = w_router.shape[1]
    local_count = experts // group_size
    old_count = old_in.shape[0]
    capacity = max(4, seq_len // experts)
    buffer_size = experts * capacity
    score_scale = 1.0 / math.sqrt(HEAD_DIM)
    length = lengths[0]
    route_row = routes[0]
    block_rows = min(512, seq_len)
    blocks = seq_len // block_rows
    normed1, back_norm1 = jax.vjp(layer_norm, inputs, ln1_gain, ln1_bias)
    normed1_low = normed1.astype(jnp.bfloat16)
    qkv_low = jnp.dot(normed1_low, w_qkv, preferred_element_type=jnp.float32).astype(jnp.bfloat16)
    queries = qkv_low[:, :model_width].reshape(seq_len, HEADS, HEAD_DIM)
    key_rows = qkv_low[:, model_width : 2 * model_width].reshape(seq_len, HEADS, HEAD_DIM)
    value_rows = qkv_low[:, 2 * model_width :].reshape(seq_len, HEADS, HEAD_DIM)
    key_pos = jnp.arange(seq_len, dtype=jnp.int32)

    def block_scores(row_start, query_block):
        raw_scores = (
            jnp.einsum("qhd,khd->hqk", query_block, key_rows, preferred_element_type=jnp.float32)
            * score_scale
        )
        query_pos = row_start + jnp.arange(query_block.shape[0], dtype=jnp.int32)
        allowed = (key_pos[None, :] <= query_pos[:, None]) & (key_pos[None, :] < length)
        return jnp.where(allowed[None], raw_scores, masked_value)

    mixed_parts = []
    lse_parts = []
    for block_index in range(blocks):
        row_start = block_index * block_rows
        scores = block_scores(row_start, queries[row_start : row_start + block_rows])
        row_max = jnp.max(scores, axis=-1, keepdims=True)
        exp_scores = jnp.exp(scores - row_max)
        row_total = jnp.sum(exp_scores, axis=-1, keepdims=True)
        prob_low = (exp_scores / row_total).astype(jnp.bfloat16)
        mixed_parts.append(
            jnp.einsum(
                "hqk,khd->qhd", prob_low, value_rows, preferred_element_type=jnp.float32
            ).astype(jnp.bfloat16)
        )
        lse_parts.append(row_max + jnp.log(row_total))
    mixed_rows = jnp.concatenate(mixed_parts, axis=0).reshape(seq_len, model_width)
    residual = inputs + jnp.dot(mixed_rows, w_proj, preferred_element_type=jnp.float32)
    normed2, back_norm2 = jax.vjp(layer_norm, residual, ln2_gain, ln2_bias)
    normed2_low = normed2.astype(jnp.bfloat16)
    logits = jnp.dot(normed2_low, w_router, preferred_element_type=jnp.float32)
    gate_vals = jax.nn.softmax(jnp.take_along_axis(logits, route_row, axis=1), axis=-1)
    pair_rank, kept_pair = rank_pairs(route_row, length, experts, capacity)
    slot_index = buffer_row(route_row, experts, group_size) * capacity + pair_rank
    target = jnp.where(kept_pair, slot_index, buffer_size).reshape(-1)
    token_ids = jnp.broadcast_to(
        jnp.arange(seq_len, dtype=jnp.int32)[:, None], (seq_len, 2)
    ).reshape(-1)
    source_token = jnp.zeros((buffer_size,), jnp.int32).at[target].set(token_ids, mode="drop")
    slot_gate = (
        jnp.zeros((buffer_size,), jnp.float32).at[target].set(gate_vals.reshape(-1), mode="drop")
    )
    slot_filled = jnp.zeros((buffer_size,), jnp.bool_).at[target].set(True, mode="drop")
    pick_index = jnp.where(kept_pair, slot_index, 0)
    kept_weight = kept_pair.astype(jnp.float32)
    zero_low = jnp.zeros((), jnp.bfloat16)
    send_rows = jnp.where(slot_filled[:, None], normed2_low[source_token], zero_low)
    send_rows = send_rows.reshape(group_size, local_count, capacity, model_width)
    received = lax.all_to_all(send_rows, "expert", split_axis=0, concat_axis=0, tiled=True)
    gathered = (
        lax.all_gather(old_in, "batch", axis=1, tiled=True),
        lax.all_gather(old_out, "batch", axis=1, tiled=True),
        lax.all_gather(new_in, "batch", axis=1, tiled=True),
        lax.all_gather(new_out, "batch", axis=1, tiled=True),
    )
    old_rows = received[:, :old_count]
    new_rows = received[:, old_count:]
    old_pre, old_hid = expert_hidden(old_rows, gathered[0])
    new_pre, new_hid = expert_hidden(new_rows, gathered[2])
    expert_result = jnp.concatenate(
        [expert_output(old_hid, gathered[1]), expert_output(new_hid, gathered[3])], axis=1
    ).astype(jnp.bfloat16)
    returned = lax.all_to_all(
        expert_result, "expert", split_axis=0, concat_axis=0, tiled=True
    ).reshape(buffer_size, model_width)
    picked = returned[pick_index].astype(jnp.float32)
    mixture = jnp.sum((gate_vals * kept_weight)[:, :, None] * picked, axis=1)
    output = residual + mixture
    grad_out = cotangent[0].astype(jnp.float32)
    gate_grad = kept_weight * jnp.sum(grad_out[:, None, :] * picked, axis=-1)
    dchosen = gate_vals * (gate_grad - jnp.sum(gate_vals * gate_grad, axis=-1, keepdims=True))
    columns = jnp.arange(experts, dtype=jnp.int32)
    dlogits = jnp.sum(
        (route_row[:, :, None] == columns[None, None, :]).astype(jnp.float32) * dchosen[:, :, None],
        axis=1,
    ).astype(jnp.bfloat16)
    send_grads = jnp.where(
        slot_filled[:, None],
        (slot_gate[:, None] * grad_out[source_token]).astype(jnp.bfloat16),
        zero_low,
    )
    send_grads = send_grads.reshape(group_size, local_count, capacity, model_width)
    arrived = lax.all_to_all(send_grads, "expert", split_axis=0, concat_axis=0, tiled=True)
    weights_back = (
        lax.all_gather(old_in, "batch", axis=1, tiled=True),
        lax.all_gather(old_out, "batch", axis=1, tiled=True),
        lax.all_gather(new_in, "batch", axis=1, tiled=True),
        lax.all_gather(new_out, "batch", axis=1, tiled=True),
    )
    old_pre, old_hid = expert_hidden(old_rows, weights_back[0])
    new_pre, new_hid = expert_hidden(new_rows, weights_back[2])
    old_dout = arrived[:, :old_count]
    new_dout = arrived[:, old_count:]
    old_dpre = expert_back(old_pre, old_dout, weights_back[1])
    new_dpre = expert_back(new_pre, new_dout, weights_back[3])
    new_out_local = jnp.einsum(
        "slcf,slcd->lfd", new_hid, new_dout, preferred_element_type=jnp.float32
    )
    new_in_local = jnp.einsum(
        "slcd,slcf->ldf", new_rows, new_dpre, preferred_element_type=jnp.float32
    )
    row_grads = jnp.concatenate(
        [row_grads_of(old_dpre, weights_back[0]), row_grads_of(new_dpre, weights_back[2])], axis=1
    ).astype(jnp.bfloat16)
    returned_grads = lax.all_to_all(
        row_grads, "expert", split_axis=0, concat_axis=0, tiled=True
    ).reshape(buffer_size, model_width)
    new_in_grad, new_out_grad = (
        lax.psum_scatter(new_in_local, "batch", scatter_dimension=1, tiled=True),
        lax.psum_scatter(new_out_local, "batch", scatter_dimension=1, tiled=True),
    )
    dnormed2 = jnp.sum(
        kept_weight[:, :, None] * returned_grads[pick_index].astype(jnp.float32), axis=1
    )
    dnormed2 = dnormed2 + jnp.dot(dlogits, w_router.T, preferred_element_type=jnp.float32)
    router_local = jnp.dot(normed2_low.T, dlogits, preferred_element_type=jnp.float32)
    dresid_norm, gain2_local, bias2_local = back_norm2(dnormed2)
    dresid = grad_out + dresid_norm
    attn_grad = dresid.astype(jnp.bfloat16)
    proj_local = jnp.dot(mixed_rows.T, attn_grad, preferred_element_type=jnp.float32)
    dmixed = (
        jnp.dot(attn_grad, w_proj.T, preferred_element_type=jnp.float32)
        .astype(jnp.bfloat16)
        .reshape(seq_len, HEADS, HEAD_DIM)
    )
    key_grads = jnp.zeros((seq_len, HEADS, HEAD_DIM), jnp.float32)
    value_grads = jnp.zeros((seq_len, HEADS, HEAD_DIM), jnp.float32)
    dquery_parts = []
    for block_index in range(blocks):
        row_start = block_index * block_rows
        query_block = queries[row_start : row_start + block_rows]
        grad_block = dmixed[row_start : row_start + block_rows]
        scores = block_scores(row_start, query_block)
        probs = jnp.exp(scores - lse_parts[block_index])
        dprobs = jnp.einsum(
            "qhd,khd->hqk", grad_block, value_rows, preferred_element_type=jnp.float32
        )
        dscores = (probs * (dprobs - jnp.sum(probs * dprobs, axis=-1, keepdims=True))).astype(
            jnp.bfloat16
        )
        dquery_parts.append(
            jnp.einsum("hqk,khd->qhd", dscores, key_rows, preferred_element_type=jnp.float32)
            * score_scale
        )
        key_grads = (
            key_grads
            + jnp.einsum("hqk,qhd->khd", dscores, query_block, preferred_element_type=jnp.float32)
            * score_scale
        )
        value_grads = value_grads + jnp.einsum(
            "hqk,qhd->khd",
            probs.astype(jnp.bfloat16),
            grad_block,
            preferred_element_type=jnp.float32,
        )
    query_grads = jnp.concatenate(dquery_parts, axis=0)
    qkv_grads = jnp.concatenate(
        [
            query_grads.reshape(seq_len, model_width),
            key_grads.reshape(seq_len, model_width),
            value_grads.reshape(seq_len, model_width),
        ],
        axis=1,
    ).astype(jnp.bfloat16)
    qkv_local = jnp.dot(normed1_low.T, qkv_grads, preferred_element_type=jnp.float32)
    dnormed1 = jnp.dot(qkv_grads, w_qkv.T, preferred_element_type=jnp.float32)
    dinput_norm, gain1_local, bias1_local = back_norm1(dnormed1)
    input_grad = dresid + dinput_norm
    summed = lax.psum(
        (qkv_local, proj_local, router_local, gain1_local, bias1_local, gain2_local, bias2_local),
        ("expert", "batch"),
    )
    return (
        output[None],
        input_grad[None],
        summed[3],
        summed[4],
        summed[5],
        summed[6],
        summed[0],
        summed[1],
        summed[2],
        new_in_grad,
        new_out_grad,
    )


def solution(mesh):
    placed = (
        P(("expert", "batch"), None, None),
        P(("expert", "batch")),
        P(("expert", "batch"), None, None),
        P(),
        P(),
        P(),
        P(),
        P(),
        P(),
        P(),
        P("expert", "batch", None),
        P("expert", "batch", None),
        P("expert", "batch", None),
        P("expert", "batch", None),
        P(("expert", "batch"), None, None),
    )
    return jax.shard_map(
        body,
        mesh=mesh,
        in_specs=placed,
        out_specs=(
            P(("expert", "batch"), None, None),
            P(("expert", "batch"), None, None),
            P(),
            P(),
            P(),
            P(),
            P(),
            P(),
            P(),
            P("expert", "batch", None),
            P("expert", "batch", None),
        ),
        check_vma=False,
    )
```

profile of v0, /device:TPU:0, one launch (start us, length us, event | category | flops | bytes accessed | tf_op | source)
XLA Modules:
  0.0 1011.6 jit_solution(11103398749579291212)
XLA Ops:
  44.8 9.4 scatter_custom_fusion
  66.8 15.3 %fusion.13 = (f32[12,512]{1,0:T(8,128)S(1)}, f32[12,512,1024]{2,1,0:T(8,128)}) fusion(pred[512,1024]{1,0:T(8,128)(4,1)} %get-tuple-element.111, bf16[512,12,64]{0,2,1:T(8,128)(2,1)} %bitcast.415, bf16[1024,12,64]{0,2,1:T(8,128)(2,1)} %bitcast.406), kind=kOutput, calls=%fused_computation.37 | convolution fusion | flops 824174592 | bytes 28073984 | tf_op jit(solution)/shard_map/qhd,khd->hqk/dot_general | solution.py:114
  82.1 12.5 %fusion.1 = f32[12,512]{1,0:T(8,128)S(1)} fusion(f32[12,512]{1,0:T(8,128)S(1)} %get-tuple-element.112, f32[12,512,1024]{2,1,0:T(8,128)} %get-tuple-element.113, pred[512,1024]{1,0:T(8,128)(4,1)S(1)} %copy-done.17), kind=kLoop, calls=%fused_computation.21 | loop fusion | flops 25159680 | bytes 25739264 | tf_op jit(solution)/shard_map/reduce_sum | solution.py:128
  97.8 9.8 fusion.126
  107.6 12.4 %fusion.12 = (f32[12,512]{1,0:T(8,128)S(1)}, f32[12,512,1024]{2,1,0:T(8,128)}) fusion(pred[512,1024]{1,0:T(8,128)(4,1)} %get-tuple-element.110, bf16[512,12,64]{0,2,1:T(8,128)(2,1)} %bitcast.417, bf16[1024,12,64]{0,2,1:T(8,128)(2,1)S(1)} %bitcast.407), kind=kOutput, calls=%fused_computation.36 | convolution fusion | flops 824174592 | bytes 28073984 | tf_op jit(solution)/shard_map/qhd,khd->hqk/dot_general | solution.py:114
  120.0 14.2 %fusion = f32[12,512]{1,0:T(8,128)S(1)} fusion(f32[12,512]{1,0:T(8,128)S(1)} %get-tuple-element.114, f32[12,512,1024]{2,1,0:T(8,128)} %get-tuple-element.115, pred[512,1024]{1,0:T(8,128)(4,1)} %get-tuple-element.110), kind=kLoop, calls=%fused_computation.20 | loop fusion | flops 25159680 | bytes 25739264 | tf_op jit(solution)/shard_map/reduce_sum | solution.py:128
  136.3 9.6 fusion.125
  152.3 8.7 scatter_custom_fusion.1
  183.4 13.8 %gather_fusion.4 = f32[2048]{0:T(1024)S(1)} fusion(f32[1024,8]{0,1:T(8,128)} %fusion.196, s32[2048]{0:T(1024)S(1)} %reshape.475), kind=kCustom, calls=%fused_computation.4 | custom fusion | bytes 32768 | tf_op jit(solution)/shard_map/jit(take_along_axis)/gather | solution.py:141
  238.3 43.2 %all_to_all.20 = bf16[4,2,128,768]{3,2,1,0:T(8,128)(2,1)} all-to-all(bf16[4,2,128,768]{3,2,1,0:T(8,128)(2,1)S(1)} %get-tuple-element.109), channel_id=1, replica_groups=mesh['expert'=4,'batch'=8] {'expert'}, dimensions={0} | all-to-all | bytes 3145728 | tf_op jit(solution)/shard_map/all_to_all | solution.py:158
  301.9 8.8 fusion.108
  326.8 9.6 fusion.19
  347.4 10.6 %fusion.127 = bf16[4,1,128,768]{3,2,0,1:T(8,128)(2,1)S(1)} fusion(bf16[1,768,3072]{2,1,0:T(8,128)(2,1)} %all-gather.5.cloned.1.call-done, f32[4,128,3072]{2,1,0:T(8,128)} %fusion.52, f32[4,128,3072]{2,1,0:T(8,128)S(1)} %fusion.46), kind=kOutput, calls=%fused_computation.163 | convolution fusion | flops 2454061056 | bytes 18087936 | tf_op jit(solution)/shard_map/slcf,ldf->slcd/dot_general | solution.py:70
  379.6 12.1 %gather_fusion.1 = bf16[2048,768]{1,0:T(8,128)(2,1)} fusion(bf16[1024,768]{1,0:T(8,128)(2,1)} %bitcast.47, s32[2048]{0:T(1024)S(1)} %broadcast_clamp_fusion), kind=kCustom, calls=%fused_computation.1 | custom fusion | bytes 6299648 | tf_op jit(solution)/shard_map/gather | solution.py:175
  391.7 12.6 %all-to-all-done.3 = bf16[4,2,128,768]{3,2,1,0:T(8,128)(2,1)} async-done(((bf16[4,2,128,768]{3,2,1,0:T(8,128)(2,1)}), bf16[4,2,128,768]{3,2,1,0:T(8,128)(2,1)}, u32[]{:S(2)}, u32[]{:S(2)}) %all-to-all-start.3) | async-done | bytes 1572896 | tf_op jit(solution)/shard_map/all_to_all | solution.py:214
  404.3 11.7 %gather_fusion.3 = bf16[2048,768]{1,0:T(8,128)(2,1)} fusion(bf16[1024,768]{1,0:T(8,128)(2,1)} %bitcast.73, s32[2048]{0:T(1024)S(1)} %broadcast_clamp_fusion), kind=kCustom, calls=%fused_computation.3 | custom fusion | bytes 6299648 | tf_op jit(solution)/shard_map/gather | solution.py:222
  423.8 11.2 %multiply_reduce_fusion.3 = f32[1024,768]{1,0:T(8,128)} fusion(f32[1024,2,768]{2,1,0:T(2,128)} %reshape.513, f32[1024,2]{1,0:T(8,128)} %copy.192), kind=kLoop, calls=%fused_computation.73 | loop fusion | flops 2359296 | bytes 9445376 | tf_op jit(solution)/shard_map/reduce_sum | solution.py:221
  446.3 17.2 %multiply_reduce_fusion.2 = (f32[1024,2]{1,0:T(8,128)}, f32[1024,768]{1,0:T(8,128)}) fusion(f32[1024,2,768]{2,1,0:T(2,128)} %reshape.512, f32[1024,768]{1,0:T(8,128)} %copy.196, f32[1024,2]{1,0:T(8,128)} %copy.183), kind=kLoop, calls=%fused_computation.72 | loop fusion | flops 5502976 | bytes 12599296 | tf_op jit(solution)/shard_map/reduce_sum | solution.py:179
  491.6 18.9 %multiply_reduce_fusion.1 = (f32[12,512]{1,0:T(8,128)}, f32[12,512,1024]{2,1,0:T(8,128)}) fusion(f32[12,512]{1,0:T(8,128)} %log_add_fusion.1, f32[12,512,1024]{2,1,0:T(8,128)} %get-tuple-element.115, pred[512,1024]{1,0:T(8,128)(4,1)} %get-tuple-element.110, bf16[512,12,64]{0,2,1:T(8,128)(2,1)} %bitcast.422, bf16[1024,12,64]{0,2,1:T(8,128)(2,1)} %bitcast.412), kind=kOutput, calls=%fused_computation.12 | convolution fusion | flops 836757504 | bytes 53264384 | tf_op jit(solution)/shard_map/qhd,khd->hqk/dot_general | solution.py:244
  510.5 22.7 %multiply_convert_fusion.1 = bf16[12,512,1024]{2,1,0:T(8,128)(2,1)} fusion(f32[12,512,1024]{2,1,0:T(8,128)} %get-tuple-element.120, f32[12,512]{1,0:T(8,128)} %get-tuple-element.119, f32[12,512]{1,0:T(8,128)} %log_add_fusion.1, f32[12,512,1024]{2,1,0:T(8,128)} %get-tuple-element.115, pred[512,1024]{1,0:T(8,128)(4,1)} %get-tuple-element.110), kind=kLoop, calls=%fused_computation.11 | loop fusion | flops 37748736 | bytes 63488000 | tf_op jit(solution)/shard_map/convert_element_type | solution.py:247
  533.2 9.5 fusion.123
  551.4 13.1 %fusion.4 = f32[12,64,1024]{2,1,0:T(8,128)} fusion(bf16[512,12,64]{0,2,1:T(8,128)(2,1)S(1)} %bitcast.425, f32[12,512]{1,0:T(8,128)S(1)} %copy-done.36, f32[12,512,1024]{2,1,0:T(8,128)} %get-tuple-element.113, pred[512,1024]{1,0:T(8,128)(4,1)S(1)} %copy-done.18), kind=kOutput, calls=%fused_computation.24 | convolution fusion | flops 830472192 | bytes 29646848 | tf_op jit(solution)/shard_map/hqk,qhd->khd/dot_general | solution.py:259
  564.4 18.9 %multiply_reduce_fusion = (f32[12,512]{1,0:T(8,128)}, f32[12,512,1024]{2,1,0:T(8,128)}) fusion(f32[12,512]{1,0:T(8,128)} %log_add_fusion, f32[12,512,1024]{2,1,0:T(8,128)} %get-tuple-element.113, pred[512,1024]{1,0:T(8,128)(4,1)} %get-tuple-element.111, bf16[512,12,64]{0,2,1:T(8,128)(2,1)} %bitcast.424, bf16[1024,12,64]{0,2,1:T(8,128)(2,1)} %bitcast.413), kind=kOutput, calls=%fused_computation.9 | convolution fusion | flops 836757504 | bytes 53264384 | tf_op jit(solution)/shard_map/qhd,khd->hqk/dot_general | solution.py:244
  583.3 13.2 %add_convert_fusion = bf16[12,64,1024]{2,1,0:T(8,128)(2,1)S(1)} fusion(f32[12,64,1024]{2,1,0:T(8,128)} %fusion.4, bf16[512,12,64]{0,2,1:T(8,128)(2,1)} %bitcast.423, f32[12,512]{1,0:T(8,128)} %log_add_fusion.1, f32[12,512,1024]{2,1,0:T(8,128)} %get-tuple-element.115, pred[512,1024]{1,0:T(8,128)(4,1)} %get-tuple-element.110), kind=kOutput, calls=%fused_computation.122 | convolution fusion | flops 832045056 | bytes 31219712 | tf_op jit(solution)/shard_map/hqk,qhd->khd/dot_general | solution.py:259
  596.6 21.9 %multiply_convert_fusion = bf16[12,512,1024]{2,1,0:T(8,128)(2,1)} fusion(f32[12,512,1024]{2,1,0:T(8,128)} %get-tuple-element.122, f32[12,512]{1,0:T(8,128)S(1)} %copy-done.42, f32[12,512]{1,0:T(8,128)S(1)} %copy-done.37, f32[12,512,1024]{2,1,0:T(8,128)} %get-tuple-element.113, pred[512,1024]{1,0:T(8,128)(4,1)S(1)} %copy-done.19), kind=kLoop, calls=%fused_computation.8 | loop fusion | flops 37748736 | bytes 63488000 | tf_op jit(solution)/shard_map/convert_element_type | solution.py:247
  618.5 8.6 fusion.124
  643.8 9.9 convolution_bitcast_fusion
  666.1 8.7 fusion.195
  693.5 40.5 %all-reduce = (f32[768]{0:T(1024)}, f32[768]{0:T(1024)}, f32[768]{0:T(1024)}, f32[768]{0:T(1024)}, f32[768,8]{0,1:T(8,128)}) all-reduce(f32[768]{0:T(1024)} %get-tuple-element.81, f32[768]{0:T(1024)} %get-tuple-element.123, f32[768]{0:T(1024)} %get-tuple-element.77, ...), channel_id=1, replica_groups=mesh['expert'=4,'batch'=8] {'expert','batch'}, use_global_device_ids=true, to_apply=%region_28.29 | all-reduce | flops 9216 | bytes 73728 | tf_op jit(solution)/shard_map/psum | solution.py:278
  734.0 100.6 %all-reduce.4.cloned.1.call-done = (f32[768,2304]{1,0:T(8,128)}, f32[768,768]{1,0:T(8,128)}) async-done(((f32[768,2304]{1,0:T(8,128)}, f32[768,768]{1,0:T(8,128)}), (f32[768,2304]{1,0:T(8,128)}, f32[768,768]{1,0:T(8,128)})) %all-reduce.4.cloned.1.call-update) | async-done | bytes 9437200 | tf_op jit(solution)/shard_map/psum | solution.py:278
  834.6 80.8 %reduce-scatter.5.cloned.1.call-done = f32[1,384,768]{2,1,0:T(8,128)} async-done(((f32[1,3072,768]{2,1,0:T(8,128)}), f32[1,384,768]{2,1,0:T(8,128)}) %reduce-scatter.5.cloned.1.call-update) | async-done | bytes 1179664 | tf_op jit(solution)/shard_map/reduce_scatter | solution.py:219
  915.4 80.9 %reduce-scatter.3.cloned.1.call-done = f32[1,96,3072]{2,1,0:T(8,128)} async-done(((f32[1,768,3072]{2,1,0:T(8,128)}), f32[1,96,3072]{2,1,0:T(8,128)}) %reduce-scatter.3.cloned.1.call-update) | async-done | bytes 1179664 | tf_op jit(solution)/shard_map/reduce_scatter | solution.py:218
  (284 shorter events, 304.6 us)
Async XLA Ops:
  7.2 10.3 %copy-start = (bf16[768,2304]{1,0:T(8,128)(2,1)S(1)}, bf16[768,2304]{1,0:T(8,128)(2,1)}, u32[]{:S(2)}) copy-start(bf16[768,2304]{1,0:T(8,128)(2,1)} %param.22) | copy-start | bytes 10616836
  7.2 279.0 %all-gather.9.cloned.1.call-start = ((), (), s32[]{:S(2)}) async-start(), calls=%async_computation.8 | async-start | bytes 5308416 | tf_op jit(solution)/shard_map/all_gather | solution.py:162
  7.9 286.1 %all-gather.5.cloned.1.call-start = ((), (), s32[]{:S(2)}) async-start(), calls=%async_computation.6 | async-start | bytes 5308416 | tf_op jit(solution)/shard_map/all_gather | solution.py:160
  8.7 293.2 %all-gather.11.cloned.1.call-start = ((), (), s32[]{:S(2)}) async-start(), calls=%async_computation.9 | async-start | bytes 5308416 | tf_op jit(solution)/shard_map/all_gather | solution.py:163
  9.4 301.3 %all-gather.7.cloned.1.call-start = ((), (), s32[]{:S(2)}) async-start(), calls=%async_computation.7 | async-start | bytes 5308416 | tf_op jit(solution)/shard_map/all_gather | solution.py:161
  66.8 15.3 %copy-start.17 = (pred[512,1024]{1,0:T(8,128)(4,1)S(1)}, pred[512,1024]{1,0:T(8,128)(4,1)}, u32[]{:S(2)}) copy-start(pred[512,1024]{1,0:T(8,128)(4,1)} %get-tuple-element.111) | copy-start | bytes 1572868
  82.1 12.5 %copy-start.34 = (f32[12,512]{1,0:T(8,128)}, f32[12,512]{1,0:T(8,128)S(1)}, u32[]{:S(2)}) copy-start(f32[12,512]{1,0:T(8,128)S(1)} %get-tuple-element.112) | copy-start | bytes 73732
  82.1 15.7 %copy-start.1 = (f32[12,512,1024]{2,1,0:T(8,128)S(1)}, f32[12,512,1024]{2,1,0:T(8,128)}, u32[]{:S(2)}) copy-start(f32[12,512,1024]{2,1,0:T(8,128)} %get-tuple-element.113) | copy-start | bytes 75497472
  94.6 13.0 %copy-start.43 = (f32[12,512]{1,0:T(8,128)}, f32[12,512]{1,0:T(8,128)S(1)}, u32[]{:S(2)}) copy-start(f32[12,512]{1,0:T(8,128)S(1)} %fusion.1) | copy-start | bytes 73732
  97.8 9.8 copy-start.9
  120.0 14.2 %copy-start.35 = (f32[12,512]{1,0:T(8,128)}, f32[12,512]{1,0:T(8,128)S(1)}, u32[]{:S(2)}) copy-start(f32[12,512]{1,0:T(8,128)S(1)} %get-tuple-element.114) | copy-start | bytes 73732
  120.0 16.2 %copy-start.2 = (f32[12,512,1024]{2,1,0:T(8,128)S(1)}, f32[12,512,1024]{2,1,0:T(8,128)}, u32[]{:S(2)}) copy-start(f32[12,512,1024]{2,1,0:T(8,128)} %get-tuple-element.115) | copy-start | bytes 75497472
  120.0 16.3 %copy-start.20 = (pred[512,1024]{1,0:T(8,128)(4,1)S(1)}, pred[512,1024]{1,0:T(8,128)(4,1)}, u32[]{:S(2)}) copy-start(pred[512,1024]{1,0:T(8,128)(4,1)} %get-tuple-element.110) | copy-start | bytes 1572868
  136.3 9.6 copy-start.44
  281.6 40.7 %all-to-all-start.2 = ((bf16[4,2,128,768]{3,2,1,0:T(8,128)(2,1)}), bf16[4,2,128,768]{3,2,1,0:T(8,128)(2,1)}, u32[]{:S(2)}, u32[]{:S(2)}) async-start(bf16[4,2,128,768]{3,2,1,0:T(8,128)(2,1)} %get-tuple-element.108), calls=%async_computation.2 | async-start | bytes 3145728 | tf_op jit(solution)/shard_map/all_to_all | solution.py:192
  322.3 41.2 %all-to-all-start.1 = ((bf16[4,2,128,768]{3,2,1,0:T(8,128)(2,1)}), bf16[4,2,128,768]{3,2,1,0:T(8,128)(2,1)}, u32[]{:S(2)}, u32[]{:S(2)}) async-start(bf16[4,2,128,768]{3,2,1,0:T(8,128)(2,1)} %copy.188), calls=%async_computation.1 | async-start | bytes 3145728 | tf_op jit(solution)/shard_map/all_to_all | solution.py:172
  359.4 13.8 %copy-start.41 = (pred[2,1024]{1,0:T(4,128)(4,1)S(1)}, pred[2,1024]{1,0:T(4,128)(4,1)}, u32[]{:S(2)}) copy-start(pred[2,1024]{1,0:T(4,128)(4,1)} %copy-done.40) | copy-start | bytes 6148
  359.4 13.8 %copy-start.52 = (f32[1024]{0:T(1024)S(1)}, f32[1024]{0:T(1024)}, u32[]{:S(2)}) copy-start(f32[1024]{0:T(1024)} %copy-done.51) | copy-start | bytes 12292
  363.4 40.9 %all-to-all-start.3 = ((bf16[4,2,128,768]{3,2,1,0:T(8,128)(2,1)}), bf16[4,2,128,768]{3,2,1,0:T(8,128)(2,1)}, u32[]{:S(2)}, u32[]{:S(2)}) async-start(bf16[4,2,128,768]{3,2,1,0:T(8,128)(2,1)} %copy.199), calls=%async_computation.3 | async-start | bytes 3145728 | tf_op jit(solution)/shard_map/all_to_all | solution.py:214
  367.8 466.8 %all-reduce.4.cloned.1.call-start = ((), (), s32[]{:S(2)}) async-start(), calls=%async_computation.12 | async-start | bytes 18874368 | tf_op jit(solution)/shard_map/psum | solution.py:278
  446.3 20.5 %copy-start.33 = (s32[1,1024,2]{1,2,0:T(2,128)S(1)}, s32[1,1024,2]{1,2,0:T(2,128)}, u32[]{:S(2)}) copy-start(s32[1,1024,2]{1,2,0:T(2,128)} %param.17) | copy-start | bytes 24580
  446.3 20.6 %copy-start.46 = (f32[1024]{0:T(1024)S(1)}, f32[1024]{0:T(1024)}, u32[]{:S(2)}) copy-start(f32[1024]{0:T(1024)} %copy-done.45) | copy-start | bytes 12292
  510.5 22.7 %copy-start.10 = (bf16[1024,768]{0,1:T(8,128)(2,1)S(1)}, bf16[1024,768]{0,1:T(8,128)(2,1)}, u32[]{:S(2)}) copy-start(bf16[1024,768]{0,1:T(8,128)(2,1)} %copy.179) | copy-start | bytes 4718596
  533.2 9.5 copy-start.22
  583.3 13.3 %copy-start.19 = (pred[512,1024]{1,0:T(8,128)(4,1)S(1)}, pred[512,1024]{1,0:T(8,128)(4,1)}, u32[]{:S(2)}) copy-start(pred[512,1024]{1,0:T(8,128)(4,1)} %get-tuple-element.111) | copy-start | bytes 1572868
  583.3 13.3 %copy-start.37 = (f32[12,512]{1,0:T(8,128)S(1)}, f32[12,512]{1,0:T(8,128)}, u32[]{:S(2)}) copy-start(f32[12,512]{1,0:T(8,128)} %log_add_fusion) | copy-start | bytes 73732
  583.3 13.3 %copy-start.42 = (f32[12,512]{1,0:T(8,128)S(1)}, f32[12,512]{1,0:T(8,128)}, u32[]{:S(2)}) copy-start(f32[12,512]{1,0:T(8,128)} %get-tuple-element.121) | copy-start | bytes 73732
  596.5 37.8 %copy-start.71 = (bf16[12,64,1024]{2,1,0:T(8,128)(2,1)}, bf16[12,64,1024]{2,1,0:T(8,128)(2,1)S(1)}, u32[]{:S(2)}) copy-start(bf16[12,64,1024]{2,1,0:T(8,128)(2,1)S(1)} %add_convert_fusion) | copy-start | bytes 4718596
  596.6 21.9 %copy-start.11 = (bf16[1024,768]{0,1:T(8,128)(2,1)S(1)}, bf16[1024,768]{0,1:T(8,128)(2,1)}, u32[]{:S(2)}) copy-start(bf16[1024,768]{0,1:T(8,128)(2,1)} %copy.179) | copy-start | bytes 4718596
  618.5 8.7 copy-start.21
  643.8 271.7 %reduce-scatter.5.cloned.1.call-start = ((), (), s32[]{:S(2)}) async-start(), calls=%async_computation.11 | async-start | bytes 10616832 | tf_op jit(solution)/shard_map/reduce_scatter | solution.py:219
  653.7 342.7 %reduce-scatter.3.cloned.1.call-start = ((), (), s32[]{:S(2)}) async-start(), calls=%async_computation.10 | async-start | bytes 10616832 | tf_op jit(solution)/shard_map/reduce_scatter | solution.py:218
  (50 other events, 185.6 us)
Sparse Core Ops, SparseCore 0:
  9.9 41.5 all-gather.8
  53.3 38.7 all-gather.4
  94.1 38.7 all-gather.10
  134.6 38.8 all-gather.6
  643.9 190.6 all-reduce.3
  838.5 76.8 reduce-scatter.4
  919.5 76.8 reduce-scatter.2
where the time goes:
time: 1020 us; the launch traced here: 1010 us
  waiting for transfers between devices  284 us (28%)
  matrix products  264 us (26%)
  local copies, waits for them, and re-layouts  195 us (19%)
  other arithmetic  155 us (15%)
  blocking collectives  83.7 us (8%)
  between operations  16 us (2%)
  starting transfers between devices  13.9 us (1%)
    psum x1, waiting for transfers between devices, body(): lax.psum((qkv_local, proj_local, router_local, gain1_local, bias1_local,...  101 us
    reduce_scatter x1, waiting for transfers between devices, body(): lax.psum_scatter(new_in_local, 'batch', scatter_dimension=1, tiled=True)  80.9 us
    reduce_scatter x1, waiting for transfers between devices, body(): lax.psum_scatter(new_out_local, 'batch', scatter_dimension=1, tiled=True)  80.8 us
    convert_element_type x2, other arithmetic, body(): (probs * (dprobs - jnp.sum(probs * dprobs, axis=-1, keepdims=True))).asty...  44.6 us
    all_to_all x1, blocking collectives, body(): lax.all_to_all(send_rows, 'expert', split_axis=0, concat_axis=0, tiled=True)  43.2 us
    psum x1, blocking collectives, body(): lax.psum((qkv_local, proj_local, router_local, gain1_local, bias1_local,...  40.5 us
    dot_general x2, matrix products, body(): jnp.einsum('qhd,khd->hqk', grad_block, value_rows, preferred_element_type...  37.7 us
    unnamed x154, local copies, waits for them, and re-layouts  37.1 us
  transfers between devices with their start and end apart: 10, of which 6 were waited for; matrix products, arithmetic and copies ran while one was open for 35% of the time, Pallas kernels for 0%

commit v1 on v0

--- a/solution.py
+++ b/solution.py
@@ -1,3 +1,4 @@
+import functools
 import math
 import jax
 import jax.numpy as jnp
@@ -8,6 +9,33 @@
 HEAD_DIM = 64
 norm_eps = 1e-05
 masked_value = -1e30
+
+
+def ends_build(point, dim_at, own_rows):
+    shaped, spare = (point.shape[:dim_at], point.shape[dim_at + 1 :])
+    return jnp.moveaxis(point.reshape(*shaped, own_rows, -1, *spare), dim_at, 0)
+
+
+def draft_sheet_on_mesh(a0, d0):
+    finding = list(a0.shape[1:])
+    finding[d0] *= a0.shape[0]
+    return jnp.moveaxis(a0, 0, d0).reshape(finding)
+
+
+def _mark_stages_all(original, axis_tag, page, patch):
+    local_part, heard = (lax.axis_size(axis_tag), lax.axis_index(axis_tag))
+    res = ends_build(original, page, local_part)
+    bank = [res[heard]]
+    for j0 in range(1, local_part):
+        r1 = res[heard ^ j0]
+        bank.append(
+            lax.ppermute(r1, axis_name=axis_tag, perm=[(w, w ^ j0) for w in range(local_part)])
+        )
+    res = jnp.stack(bank, axis=0)[heard ^ jnp.arange(local_part)]
+    return draft_sheet_on_mesh(res, patch)
+
+
+save_lines_now = functools.partial(_mark_stages_all, axis_tag="expert", page=0, patch=0)
 
 
 def layer_norm(field_in, gain_vec, bias_vec):
@@ -155,7 +183,7 @@
     zero_low = jnp.zeros((), jnp.bfloat16)
     send_rows = jnp.where(slot_filled[:, None], normed2_low[source_token], zero_low)
     send_rows = send_rows.reshape(group_size, local_count, capacity, model_width)
-    received = lax.all_to_all(send_rows, "expert", split_axis=0, concat_axis=0, tiled=True)
+    received = save_lines_now(send_rows)
     gathered = (
         lax.all_gather(old_in, "batch", axis=1, tiled=True),
         lax.all_gather(old_out, "batch", axis=1, tiled=True),

time: 1020 us -> 995 us (0.975)
  blocking collectives: 83.7 us -> 40.6 us
    all_to_all x1 -> x0, blocking collectives: 43.2 us -> none  [body(): lax.all_to_all(send_rows, 'expert', split_axis=0, concat_axis=0, tiled=True)]
    unnamed x154 -> x164, local copies, waits for them, and re-layouts: 37.1 us -> 38 us
  transfers between devices with their start and end apart: 10 -> 13, of which waited for: 6 -> 5; matrix products, arithmetic and copies ran while one was open for 35% -> 37% of each run, Pallas kernels for 0% -> 0%
where the time goes in v1:
time: 995 us; the launch traced here: 983 us
  waiting for transfers between devices  280 us (28%)
  matrix products  264 us (27%)
  local copies, waits for them, and re-layouts  203 us (20%)
  other arithmetic  160 us (16%)
  blocking collectives  40.6 us (4%)
  starting transfers between devices  20.7 us (2%)
  between operations  16 us (2%)
    psum x1, waiting for transfers between devices, body(): lax.psum((qkv_local, proj_local, router_local, gain1_local, bias1_local,...  100 us
    reduce_scatter x1, waiting for transfers between devices, body(): lax.psum_scatter(new_in_local, 'batch', scatter_dimension=1, tiled=True)  80.9 us
    reduce_scatter x1, waiting for transfers between devices, body(): lax.psum_scatter(new_out_local, 'batch', scatter_dimension=1, tiled=True)  80.8 us
    convert_element_type x2, other arithmetic, body(): (probs * (dprobs - jnp.sum(probs * dprobs, axis=-1, keepdims=True))).asty...  44.6 us
    psum x1, blocking collectives, body(): lax.psum((qkv_local, proj_local, router_local, gain1_local, bias1_local,...  40.6 us
    unnamed x164, local copies, waits for them, and re-layouts  38 us
    dot_general x2, matrix products, body(): jnp.einsum('qhd,khd->hqk', grad_block, value_rows, preferred_element_type...  37.6 us
    dot_general x2, matrix products, block_scores(): jnp.einsum('qhd,khd->hqk', query_block, key_rows, preferred_element_type=...  26.9 us
  transfers between devices with their start and end apart: 13, of which 5 were waited for; matrix products, arithmetic and copies ran while one was open for 37% of the time, Pallas kernels for 0%

profile of v1, /device:TPU:0, one launch (start us, length us, event | category | flops | bytes accessed | tf_op | source)
XLA Modules:
  0.0 983.5 jit_solution(8285075350827354128)
XLA Ops:
  46.1 14.9 %fusion.13 = (f32[12,512]{1,0:T(8,128)S(1)}, f32[12,512,1024]{2,1,0:T(8,128)}) fusion(pred[512,1024]{1,0:T(8,128)(4,1)S(1)} %get-tuple-element.113, bf16[512,12,64]{0,2,1:T(8,128)(2,1)} %bitcast.428, bf16[1024,12,64]{0,2,1:T(8,128)(2,1)} %bitcast.419), kind=kOutput, calls=%fused_computation.38 | convolution fusion | flops 824174592 | bytes 28073984 | tf_op jit(solution)/shard_map/qhd,khd->hqk/dot_general | solution.py:142
  61.0 12.5 %fusion.1 = f32[12,512]{1,0:T(8,128)S(1)} fusion(f32[12,512]{1,0:T(8,128)S(1)} %get-tuple-element.114, f32[12,512,1024]{2,1,0:T(8,128)} %get-tuple-element.115, pred[512,1024]{1,0:T(8,128)(4,1)S(1)} %get-tuple-element.113), kind=kLoop, calls=%fused_computation.22 | loop fusion | flops 25159680 | bytes 25739264 | tf_op jit(solution)/shard_map/reduce_sum | solution.py:156
  77.3 10.0 %fusion.126 = bf16[512,12,64]{0,2,1:T(8,128)(2,1)} fusion(bf16[1024,12,64]{0,2,1:T(8,128)(2,1)} %bitcast.423, f32[12,512]{1,0:T(8,128)S(1)} %fusion.1, f32[12,512]{1,0:T(8,128)S(1)} %get-tuple-element.114, f32[12,512,1024]{2,1,0:T(8,128)S(1)} %copy-done.1, pred[512,1024]{1,0:T(8,128)(4,1)} %copy-done.17), kind=kOutput, calls=%fused_computation.164 | convolution fusion | flops 837156864 | bytes 28098560 | tf_op jit(solution)/shard_map/hqk,khd->qhd/dot_general | solution.py:159
  87.3 12.0 %fusion.12 = (f32[12,512]{1,0:T(8,128)S(1)}, f32[12,512,1024]{2,1,0:T(8,128)}) fusion(pred[512,1024]{1,0:T(8,128)(4,1)} %get-tuple-element.112, bf16[512,12,64]{0,2,1:T(8,128)(2,1)} %bitcast.430, bf16[1024,12,64]{0,2,1:T(8,128)(2,1)S(1)} %bitcast.420), kind=kOutput, calls=%fused_computation.37 | convolution fusion | flops 824174592 | bytes 28073984 | tf_op jit(solution)/shard_map/qhd,khd->hqk/dot_general | solution.py:142
  99.3 14.2 %fusion = f32[12,512]{1,0:T(8,128)S(1)} fusion(f32[12,512]{1,0:T(8,128)S(1)} %get-tuple-element.116, f32[12,512,1024]{2,1,0:T(8,128)} %get-tuple-element.117, pred[512,1024]{1,0:T(8,128)(4,1)} %get-tuple-element.112), kind=kLoop, calls=%fused_computation.21 | loop fusion | flops 25159680 | bytes 25739264 | tf_op jit(solution)/shard_map/reduce_sum | solution.py:156
  115.8 9.9 %fusion.125 = bf16[512,12,64]{0,2,1:T(8,128)(2,1)} fusion(bf16[1024,12,64]{0,2,1:T(8,128)(2,1)} %bitcast.424, f32[12,512]{1,0:T(8,128)S(1)} %fusion, f32[12,512]{1,0:T(8,128)S(1)} %get-tuple-element.116, f32[12,512,1024]{2,1,0:T(8,128)S(1)} %copy-done.2, pred[512,1024]{1,0:T(8,128)(4,1)S(1)} %copy-done.20), kind=kOutput, calls=%fused_computation.163 | convolution fusion | flops 837156864 | bytes 28098560 | tf_op jit(solution)/shard_map/hqk,khd->qhd/dot_general | solution.py:159
  135.9 10.0 %scatter_custom_fusion = pred[1024]{0:T(1024)(128)(4,1)} fusion(s32[2048]{0:T(1024)} %bitcast.450, pred[2048]{0:T(1024)(128)(4,1)S(1)} %broadcast.370, pred[]{:T(512)} %constant.103.clone.1), kind=kCustom, calls=%fused_computation.244 | custom fusion | bytes 1536 | tf_op jit(solution)/shard_map/scatter | solution.py:180
  149.4 8.7 scatter_custom_fusion.1
  211.1 13.8 %gather_fusion.5 = f32[2048]{0:T(1024)S(1)} fusion(f32[1024,8]{0,1:T(8,128)} %fusion.197, s32[2048]{0:T(1024)S(1)} %reshape.515), kind=kCustom, calls=%fused_computation.5 | custom fusion | bytes 32768 | tf_op jit(solution)/shard_map/jit(take_along_axis)/gather | solution.py:169
  276.3 8.8 fusion.108
  299.8 9.6 fusion.19
  320.3 10.6 %fusion.127 = bf16[4,1,128,768]{3,2,0,1:T(8,128)(2,1)S(1)} fusion(bf16[1,768,3072]{2,1,0:T(8,128)(2,1)} %all-gather.5.cloned.1.call-done, f32[4,128,3072]{2,1,0:T(8,128)} %fusion.52, f32[4,128,3072]{2,1,0:T(8,128)S(1)} %fusion.46), kind=kOutput, calls=%fused_computation.165 | convolution fusion | flops 2454061056 | bytes 18087936 | tf_op jit(solution)/shard_map/slcf,ldf->slcd/dot_general | solution.py:98
  351.6 12.1 %gather_fusion.2 = bf16[2048,768]{1,0:T(8,128)(2,1)} fusion(bf16[1024,768]{1,0:T(8,128)(2,1)} %bitcast.55, s32[2048]{0:T(1024)S(1)} %broadcast_clamp_fusion), kind=kCustom, calls=%fused_computation.2 | custom fusion | bytes 6299648 | tf_op jit(solution)/shard_map/gather | solution.py:203
  363.7 12.6 %all-to-all-done.2 = bf16[4,2,128,768]{3,2,1,0:T(8,128)(2,1)} async-done(((bf16[4,2,128,768]{3,2,1,0:T(8,128)(2,1)}), bf16[4,2,128,768]{3,2,1,0:T(8,128)(2,1)}, u32[]{:S(2)}, u32[]{:S(2)}) %all-to-all-start.2) | async-done | bytes 1572896 | tf_op jit(solution)/shard_map/all_to_all | solution.py:242
  376.3 11.7 %gather_fusion.4 = bf16[2048,768]{1,0:T(8,128)(2,1)} fusion(bf16[1024,768]{1,0:T(8,128)(2,1)} %bitcast.81, s32[2048]{0:T(1024)S(1)} %broadcast_clamp_fusion), kind=kCustom, calls=%fused_computation.4 | custom fusion | bytes 6299648 | tf_op jit(solution)/shard_map/gather | solution.py:250
  395.8 11.2 %multiply_reduce_fusion.3 = f32[1024,768]{1,0:T(8,128)} fusion(f32[1024,2,768]{2,1,0:T(2,128)} %reshape.554, f32[1024,2]{1,0:T(8,128)} %copy.195), kind=kLoop, calls=%fused_computation.74 | loop fusion | flops 2359296 | bytes 9445376 | tf_op jit(solution)/shard_map/reduce_sum | solution.py:249
  418.3 17.3 %multiply_reduce_fusion.2 = (f32[1024,2]{1,0:T(8,128)}, f32[1024,768]{1,0:T(8,128)}) fusion(f32[1024,2,768]{2,1,0:T(2,128)} %reshape.553, f32[1024,768]{1,0:T(8,128)} %copy.199, f32[1024,2]{1,0:T(8,128)} %copy.186), kind=kLoop, calls=%fused_computation.73 | loop fusion | flops 5502976 | bytes 12599296 | tf_op jit(solution)/shard_map/reduce_sum | solution.py:207
  463.6 18.8 %multiply_reduce_fusion.1 = (f32[12,512]{1,0:T(8,128)}, f32[12,512,1024]{2,1,0:T(8,128)}) fusion(f32[12,512]{1,0:T(8,128)} %log_add_fusion.1, f32[12,512,1024]{2,1,0:T(8,128)} %get-tuple-element.117, pred[512,1024]{1,0:T(8,128)(4,1)} %get-tuple-element.112, bf16[512,12,64]{0,2,1:T(8,128)(2,1)} %bitcast.435, bf16[1024,12,64]{0,2,1:T(8,128)(2,1)} %bitcast.425), kind=kOutput, calls=%fused_computation.13 | convolution fusion | flops 836757504 | bytes 53264384 | tf_op jit(solution)/shard_map/qhd,khd->hqk/dot_general | solution.py:272
  482.5 22.7 %multiply_convert_fusion.1 = bf16[12,512,1024]{2,1,0:T(8,128)(2,1)} fusion(f32[12,512,1024]{2,1,0:T(8,128)} %get-tuple-element.122, f32[12,512]{1,0:T(8,128)} %get-tuple-element.121, f32[12,512]{1,0:T(8,128)} %log_add_fusion.1, f32[12,512,1024]{2,1,0:T(8,128)} %get-tuple-element.117, pred[512,1024]{1,0:T(8,128)(4,1)} %get-tuple-element.112), kind=kLoop, calls=%fused_computation.12 | loop fusion | flops 37748736 | bytes 63488000 | tf_op jit(solution)/shard_map/convert_element_type | solution.py:275
  505.2 9.5 fusion.123
  514.7 8.6 fusion.198
  523.3 13.1 %fusion.4 = f32[12,64,1024]{2,1,0:T(8,128)} fusion(bf16[512,12,64]{0,2,1:T(8,128)(2,1)S(1)} %bitcast.438, f32[12,512]{1,0:T(8,128)S(1)} %copy-done.37, f32[12,512,1024]{2,1,0:T(8,128)} %get-tuple-element.115, pred[512,1024]{1,0:T(8,128)(4,1)S(1)} %copy-done.18), kind=kOutput, calls=%fused_computation.25 | convolution fusion | flops 830472192 | bytes 29646848 | tf_op jit(solution)/shard_map/hqk,qhd->khd/dot_general | solution.py:287
  536.4 18.8 %multiply_reduce_fusion = (f32[12,512]{1,0:T(8,128)}, f32[12,512,1024]{2,1,0:T(8,128)}) fusion(f32[12,512]{1,0:T(8,128)} %log_add_fusion, f32[12,512,1024]{2,1,0:T(8,128)} %get-tuple-element.115, pred[512,1024]{1,0:T(8,128)(4,1)} %copy-done.17, bf16[512,12,64]{0,2,1:T(8,128)(2,1)} %bitcast.437, bf16[1024,12,64]{0,2,1:T(8,128)(2,1)} %bitcast.426), kind=kOutput, calls=%fused_computation.10 | convolution fusion | flops 836757504 | bytes 53264384 | tf_op jit(solution)/shard_map/qhd,khd->hqk/dot_general | solution.py:272
  555.2 13.2 %add_convert_fusion = bf16[12,64,1024]{2,1,0:T(8,128)(2,1)S(1)} fusion(f32[12,64,1024]{2,1,0:T(8,128)} %fusion.4, bf16[512,12,64]{0,2,1:T(8,128)(2,1)} %bitcast.436, f32[12,512]{1,0:T(8,128)} %log_add_fusion.1, f32[12,512,1024]{2,1,0:T(8,128)} %get-tuple-element.117, pred[512,1024]{1,0:T(8,128)(4,1)} %get-tuple-element.112), kind=kOutput, calls=%fused_computation.123 | convolution fusion | flops 832045056 | bytes 31219712 | tf_op jit(solution)/shard_map/hqk,qhd->khd/dot_general | solution.py:287
  568.5 21.8 %multiply_convert_fusion = bf16[12,512,1024]{2,1,0:T(8,128)(2,1)} fusion(f32[12,512,1024]{2,1,0:T(8,128)} %get-tuple-element.124, f32[12,512]{1,0:T(8,128)S(1)} %copy-done.43, f32[12,512]{1,0:T(8,128)S(1)} %copy-done.38, f32[12,512,1024]{2,1,0:T(8,128)} %get-tuple-element.115, pred[512,1024]{1,0:T(8,128)(4,1)S(1)} %copy-done.19), kind=kLoop, calls=%fused_computation.9 | loop fusion | flops 37748736 | bytes 63488000 | tf_op jit(solution)/shard_map/convert_element_type | solution.py:275
  590.4 8.7 fusion.124
  615.7 9.9 %convolution_bitcast_fusion = f32[1,3072,768]{2,1,0:T(8,128)} fusion(f32[4,128,3072]{2,1,0:T(8,128)} %fusion.44, bf16[4,2,128,768]{3,2,1,0:T(8,128)(2,1)} %all-to-all-done.1), kind=kOutput, calls=%fused_computation.79 | convolution fusion | flops 2430074880 | bytes 16515072 | tf_op jit(solution)/shard_map/slcf,slcd->lfd/dot_general | solution.py:233
  638.0 8.7 fusion.196
  665.5 40.6 %all-reduce = (f32[768]{0:T(1024)}, f32[768]{0:T(1024)}, f32[768]{0:T(1024)}, f32[768]{0:T(1024)}, f32[768,8]{0,1:T(8,128)}) all-reduce(f32[768]{0:T(1024)} %get-tuple-element.81, f32[768]{0:T(1024)} %get-tuple-element.125, f32[768]{0:T(1024)} %get-tuple-element.77, ...), channel_id=1, replica_groups=mesh['expert'=4,'batch'=8] {'expert','batch'}, use_global_device_ids=true, to_apply=%region_28.29 | all-reduce | flops 9216 | bytes 73728 | tf_op jit(solution)/shard_map/psum | solution.py:306
  706.1 100.4 %all-reduce.4.cloned.1.call-done = (f32[768,2304]{1,0:T(8,128)}, f32[768,768]{1,0:T(8,128)}) async-done(((f32[768,2304]{1,0:T(8,128)}, f32[768,768]{1,0:T(8,128)}), (f32[768,2304]{1,0:T(8,128)}, f32[768,768]{1,0:T(8,128)})) %all-reduce.4.cloned.1.call-update) | async-done | bytes 9437200 | tf_op jit(solution)/shard_map/psum | solution.py:306
  806.5 80.8 %reduce-scatter.5.cloned.1.call-done = f32[1,384,768]{2,1,0:T(8,128)} async-done(((f32[1,3072,768]{2,1,0:T(8,128)}), f32[1,384,768]{2,1,0:T(8,128)}) %reduce-scatter.5.cloned.1.call-update) | async-done | bytes 1179664 | tf_op jit(solution)/shard_map/reduce_scatter | solution.py:247
  887.3 80.9 %reduce-scatter.3.cloned.1.call-done = f32[1,96,3072]{2,1,0:T(8,128)} async-done(((f32[1,768,3072]{2,1,0:T(8,128)}), f32[1,96,3072]{2,1,0:T(8,128)}) %reduce-scatter.3.cloned.1.call-update) | async-done | bytes 1179664 | tf_op jit(solution)/shard_map/reduce_scatter | solution.py:246
  (305 shorter events, 311.0 us)
Async XLA Ops:
  7.2 253.4 %all-gather.9.cloned.1.call-start = ((), (), s32[]{:S(2)}) async-start(), calls=%async_computation.7 | async-start | bytes 5308416 | tf_op jit(solution)/shard_map/all_gather | solution.py:190
  7.9 260.5 %all-gather.5.cloned.1.call-start = ((), (), s32[]{:S(2)}) async-start(), calls=%async_computation.5 | async-start | bytes 5308416 | tf_op jit(solution)/shard_map/all_gather | solution.py:188
  8.7 267.6 %all-gather.11.cloned.1.call-start = ((), (), s32[]{:S(2)}) async-start(), calls=%async_computation.8 | async-start | bytes 5308416 | tf_op jit(solution)/shard_map/all_gather | solution.py:191
  9.4 275.7 %all-gather.7.cloned.1.call-start = ((), (), s32[]{:S(2)}) async-start(), calls=%async_computation.6 | async-start | bytes 5308416 | tf_op jit(solution)/shard_map/all_gather | solution.py:189
  46.1 14.9 %copy-start.17 = (pred[512,1024]{1,0:T(8,128)(4,1)}, pred[512,1024]{1,0:T(8,128)(4,1)S(1)}, u32[]{:S(2)}) copy-start(pred[512,1024]{1,0:T(8,128)(4,1)S(1)} %get-tuple-element.113) | copy-start | bytes 1572868
  61.0 12.5 %copy-start.35 = (f32[12,512]{1,0:T(8,128)}, f32[12,512]{1,0:T(8,128)S(1)}, u32[]{:S(2)}) copy-start(f32[12,512]{1,0:T(8,128)S(1)} %get-tuple-element.114) | copy-start | bytes 73732
  61.0 16.3 %copy-start.1 = (f32[12,512,1024]{2,1,0:T(8,128)S(1)}, f32[12,512,1024]{2,1,0:T(8,128)}, u32[]{:S(2)}) copy-start(f32[12,512,1024]{2,1,0:T(8,128)} %get-tuple-element.115) | copy-start | bytes 75497472
  73.5 13.8 %copy-start.44 = (f32[12,512]{1,0:T(8,128)}, f32[12,512]{1,0:T(8,128)S(1)}, u32[]{:S(2)}) copy-start(f32[12,512]{1,0:T(8,128)S(1)} %fusion.1) | copy-start | bytes 73732
  99.3 14.2 %copy-start.36 = (f32[12,512]{1,0:T(8,128)}, f32[12,512]{1,0:T(8,128)S(1)}, u32[]{:S(2)}) copy-start(f32[12,512]{1,0:T(8,128)S(1)} %get-tuple-element.116) | copy-start | bytes 73732
  99.3 16.5 %copy-start.2 = (f32[12,512,1024]{2,1,0:T(8,128)S(1)}, f32[12,512,1024]{2,1,0:T(8,128)}, u32[]{:S(2)}) copy-start(f32[12,512,1024]{2,1,0:T(8,128)} %get-tuple-element.117) | copy-start | bytes 75497472
  99.3 16.5 %copy-start.20 = (pred[512,1024]{1,0:T(8,128)(4,1)S(1)}, pred[512,1024]{1,0:T(8,128)(4,1)}, u32[]{:S(2)}) copy-start(pred[512,1024]{1,0:T(8,128)(4,1)} %get-tuple-element.112) | copy-start | bytes 1572868
  115.8 13.2 %copy-start.67 = (s32[1,8,2,128]{3,1,2,0:T(8,128)S(1)}, s32[1,8,2,128]{3,1,2,0:T(8,128)}, u32[]{:S(2)}) copy-start(s32[1,8,2,128]{3,1,2,0:T(8,128)} %copy.226) | copy-start | bytes 24580
  146.6 30.1 %copy-start.68 = (pred[4,2,128]{2,1,0:T(4,128)(4,1)}, pred[4,2,128]{2,1,0:T(4,128)(4,1)S(1)}, u32[]{:S(2)}) copy-start(pred[4,2,128]{2,1,0:T(4,128)(4,1)S(1)} %broadcast_in_dim.157) | copy-start | bytes 3076
  179.6 75.1 %collective-permute-start.2 = (bf16[1,2,128,768]{3,2,1,0:T(8,128)(2,1)}, bf16[1,2,128,768]{3,2,1,0:T(8,128)(2,1)}, u32[]{:S(2)}, u32[]{:S(2)}) collective-permute-start(bf16[1,2,128,768]{3,2,1,0:T(8,128)(2,1)} %get-tuple-element.109), channel_id=1, source_target_pairs={{0,24},{8,16},{16,8},{24,0},{1,25},{9,17},{17,9},{25,1},{2,26},{10... | collective-permute-start | bytes 1179656 | tf_op jit(solution)/shard_map/ppermute | solution.py:32
  184.2 70.4 %collective-permute-start.1 = (bf16[1,2,128,768]{3,2,1,0:T(8,128)(2,1)}, bf16[1,2,128,768]{3,2,1,0:T(8,128)(2,1)}, u32[]{:S(2)}, u32[]{:S(2)}) collective-permute-start(bf16[1,2,128,768]{3,2,1,0:T(8,128)(2,1)} %get-tuple-element.110), channel_id=1, source_target_pairs={{0,16},{8,24},{16,0},{24,8},{1,17},{9,25},{17,1},{25,9},{2,18},{10... | collective-permute-start | bytes 1179656 | tf_op jit(solution)/shard_map/ppermute | solution.py:32
  184.2 70.4 %collective-permute-start = (bf16[1,2,128,768]{3,2,1,0:T(8,128)(2,1)}, bf16[1,2,128,768]{3,2,1,0:T(8,128)(2,1)}, u32[]{:S(2)}, u32[]{:S(2)}) collective-permute-start(bf16[1,2,128,768]{3,2,1,0:T(8,128)(2,1)} %get-tuple-element.111), channel_id=1, source_target_pairs={{0,8},{8,0},{16,24},{24,16},{1,9},{9,1},{17,25},{25,17},{2,10},{10... | collective-permute-start | bytes 1179656 | tf_op jit(solution)/shard_map/ppermute | solution.py:32
  249.3 45.1 %all-to-all-start.1 = ((bf16[4,2,128,768]{3,2,1,0:T(8,128)(2,1)}), bf16[4,2,128,768]{3,2,1,0:T(8,128)(2,1)}, u32[]{:S(2)}, u32[]{:S(2)}) async-start(bf16[4,2,128,768]{3,2,1,0:T(8,128)(2,1)} %fusion.85), calls=%async_computation.1 | async-start | bytes 3145728 | tf_op jit(solution)/shard_map/all_to_all | solution.py:220
  294.5 40.9 %all-to-all-start = ((bf16[4,2,128,768]{3,2,1,0:T(8,128)(2,1)}), bf16[4,2,128,768]{3,2,1,0:T(8,128)(2,1)}, u32[]{:S(2)}, u32[]{:S(2)}) async-start(bf16[4,2,128,768]{3,2,1,0:T(8,128)(2,1)} %copy.191), calls=%async_computation | async-start | bytes 3145728 | tf_op jit(solution)/shard_map/all_to_all | solution.py:200
  332.3 12.8 %copy-start.42 = (pred[2,1024]{1,0:T(4,128)(4,1)S(1)}, pred[2,1024]{1,0:T(4,128)(4,1)}, u32[]{:S(2)}) copy-start(pred[2,1024]{1,0:T(4,128)(4,1)} %copy-done.41) | copy-start | bytes 6148
  332.3 12.8 %copy-start.53 = (f32[1024]{0:T(1024)S(1)}, f32[1024]{0:T(1024)}, u32[]{:S(2)}) copy-start(f32[1024]{0:T(1024)} %copy-done.52) | copy-start | bytes 12292
  335.3 41.0 %all-to-all-start.2 = ((bf16[4,2,128,768]{3,2,1,0:T(8,128)(2,1)}), bf16[4,2,128,768]{3,2,1,0:T(8,128)(2,1)}, u32[]{:S(2)}, u32[]{:S(2)}) async-start(bf16[4,2,128,768]{3,2,1,0:T(8,128)(2,1)} %copy.202), calls=%async_computation.2 | async-start | bytes 3145728 | tf_op jit(solution)/shard_map/all_to_all | solution.py:242
  339.7 466.8 %all-reduce.4.cloned.1.call-start = ((), (), s32[]{:S(2)}) async-start(), calls=%async_computation.11 | async-start | bytes 18874368 | tf_op jit(solution)/shard_map/psum | solution.py:306
  418.3 20.6 %copy-start.34 = (s32[1,1024,2]{1,2,0:T(2,128)S(1)}, s32[1,1024,2]{1,2,0:T(2,128)}, u32[]{:S(2)}) copy-start(s32[1,1024,2]{1,2,0:T(2,128)} %param.17) | copy-start | bytes 24580
  418.3 20.6 %copy-start.47 = (f32[1024]{0:T(1024)S(1)}, f32[1024]{0:T(1024)}, u32[]{:S(2)}) copy-start(f32[1024]{0:T(1024)} %copy-done.46) | copy-start | bytes 12292
  482.5 22.7 %copy-start.10 = (bf16[1024,768]{0,1:T(8,128)(2,1)S(1)}, bf16[1024,768]{0,1:T(8,128)(2,1)}, u32[]{:S(2)}) copy-start(bf16[1024,768]{0,1:T(8,128)(2,1)} %copy.182) | copy-start | bytes 4718596
  555.2 13.3 %copy-start.19 = (pred[512,1024]{1,0:T(8,128)(4,1)S(1)}, pred[512,1024]{1,0:T(8,128)(4,1)}, u32[]{:S(2)}) copy-start(pred[512,1024]{1,0:T(8,128)(4,1)} %copy-done.17) | copy-start | bytes 1572868
  555.2 13.3 %copy-start.38 = (f32[12,512]{1,0:T(8,128)S(1)}, f32[12,512]{1,0:T(8,128)}, u32[]{:S(2)}) copy-start(f32[12,512]{1,0:T(8,128)} %log_add_fusion) | copy-start | bytes 73732
  555.2 13.3 %copy-start.43 = (f32[12,512]{1,0:T(8,128)S(1)}, f32[12,512]{1,0:T(8,128)}, u32[]{:S(2)}) copy-start(f32[12,512]{1,0:T(8,128)} %get-tuple-element.123) | copy-start | bytes 73732
  568.5 37.8 %copy-start.76 = (bf16[12,64,1024]{2,1,0:T(8,128)(2,1)}, bf16[12,64,1024]{2,1,0:T(8,128)(2,1)S(1)}, u32[]{:S(2)}) copy-start(bf16[12,64,1024]{2,1,0:T(8,128)(2,1)S(1)} %add_convert_fusion) | copy-start | bytes 4718596
  568.5 21.9 %copy-start.11 = (bf16[1024,768]{0,1:T(8,128)(2,1)S(1)}, bf16[1024,768]{0,1:T(8,128)(2,1)}, u32[]{:S(2)}) copy-start(bf16[1024,768]{0,1:T(8,128)(2,1)} %copy.182) | copy-start | bytes 4718596
  615.7 271.7 %reduce-scatter.5.cloned.1.call-start = ((), (), s32[]{:S(2)}) async-start(), calls=%async_computation.10 | async-start | bytes 10616832 | tf_op jit(solution)/shard_map/reduce_scatter | solution.py:247
  625.6 342.6 %reduce-scatter.3.cloned.1.call-start = ((), (), s32[]{:S(2)}) async-start(), calls=%async_computation.9 | async-start | bytes 10616832 | tf_op jit(solution)/shard_map/reduce_scatter | solution.py:246
  (58 other events, 258.3 us)
Sparse Core Ops, SparseCore 0:
  9.9 41.4 all-gather.8
  53.3 38.7 all-gather.4
  94.0 38.7 all-gather.10
  134.6 38.7 all-gather.6
  615.8 190.6 all-reduce.3
  810.4 76.8 reduce-scatter.4
  891.4 76.8 reduce-scatter.2
